TPU v7x, 256 devices: a whole 4x4x8 slice. The times are simulated.
256 devices in a mesh: dp: 32 (over z, x), tensor: 8 (over y, core).
Axes of the slice: x: 4, y: 4, z: 8, core: 2. Of those that a mesh axis runs over, the one named last changes fastest.
Arguments:
- layer_input: bfloat16 [65536, 5120], P('dp', 'tensor'), may hold values from -6 to 6
- query_states: bfloat16 [65536, 5120], P('dp', 'tensor'), may hold values from -96 to 96
- key_states: bfloat16 [65536, 1024], P('dp', 'tensor'), may hold values from -12 to 12
- value_states: bfloat16 [65536, 1024], P('dp', 'tensor'), may hold values from -6 to 6
- output_grad: bfloat16 [65536, 5120], P('dp', 'tensor'), may hold values from -24 to 24
- doc_lengths: int32 [64, 8], P('dp'), may hold values from 0 to 1024, as said below
- send_order: int32 [32, 2], P('dp'), may hold values from 0 to 1, each once within a row
Outputs:
- query_grad: bfloat16 [65536, 5120], P('dp', 'tensor')
- kv_weight_grad: float32 [2048, 5120], P('dp', 'tensor')
Inputs may be any that keep to these rules, and one draw needn't show every extreme that they name: `doc_lengths`: each row's 8 lengths sum to at most 1024; the rest of the row is padding. The rows of the last index of dp are full, and the last row of all is a single document.
All inputs are finite; a program needn't handle non-finite values.
Results may differ from a plain program's by a relative error of at most 0.02.
Values may be sent and summed in bfloat16 or wider, within the bound.
A program may use at most 192 MiB of HBM per device.

v0:
```python
import jax
import jax.numpy as jnp
from jax import lax
from jax.sharding import PartitionSpec as P

QH = 40
KVH = 8
HD = 128
ROW_LEN = 1024
DOCS = 8


loss_scale = 256.0
masked_score = -1e30


def partner(value, axis, distance):
    mask = 2**distance
    pairs = [(source, source ^ mask) for source in range(lax.axis_size(axis))]
    return lax.ppermute(value, axis, pairs)


def segment_ids(doc_lengths):
    boundaries = jnp.cumsum(doc_lengths, axis=1)
    position = jnp.arange(ROW_LEN, dtype=jnp.int32)
    return jnp.sum((position[None, :, None] >= boundaries[:, None, :]).astype(jnp.int32), axis=2)


def attend_row(operands):
    query_row, key_row, value_row, grad_row, segment = operands
    local_heads = key_row.shape[1] // HD
    group_size = QH // KVH
    score_scale = HD ** (-0.5)
    block_rows = 128
    block_count = ROW_LEN // block_rows
    query_all = query_row.reshape(ROW_LEN, local_heads, group_size, HD)
    key_all = key_row.reshape(ROW_LEN, local_heads, HD)
    value_all = value_row.reshape(ROW_LEN, local_heads, HD)
    live_token = (segment < DOCS).astype(grad_row.dtype)
    grad_all = (grad_row * live_token[:, None]).reshape(ROW_LEN, local_heads, group_size, HD)
    position = jnp.arange(ROW_LEN, dtype=jnp.int32)
    stat_shape = (local_heads, group_size, block_rows, 1)
    tile_shape = (local_heads, group_size, block_rows, block_rows)
    key_parts = [
        jnp.zeros((block_rows, local_heads, HD), jnp.float32) for index in range(block_count)
    ]
    value_parts = [
        jnp.zeros((block_rows, local_heads, HD), jnp.float32) for index in range(block_count)
    ]
    pieces = []
    for query_index in range(block_count):
        q_first = query_index * block_rows
        q_last = q_first + block_rows
        query_block = query_all[q_first:q_last]
        grad_block = grad_all[q_first:q_last].transpose(1, 2, 0, 3)
        first_segment = segment[q_first]

        def tile_scores(k_first):
            key_block = key_all[k_first : k_first + block_rows]
            scores = (
                jnp.einsum(
                    "qgjd,kgd->gjqk", query_block, key_block, preferred_element_type=jnp.float32
                )
                * score_scale
            )
            allowed = (
                position[None, k_first : k_first + block_rows] <= position[q_first:q_last, None]
            ) & (segment[None, k_first : k_first + block_rows] == segment[q_first:q_last, None])
            return jnp.where(allowed, scores, masked_score)

        live_tiles = []
        for key_index in range(query_index + 1):
            k_first = key_index * block_rows
            live_tiles.append(
                (first_segment < DOCS) & (segment[k_first + block_rows - 1] >= first_segment)
            )
        running_max = jnp.full(stat_shape, masked_score, jnp.float32)
        running_sum = jnp.zeros(stat_shape, jnp.float32)
        for key_index in range(query_index + 1):
            k_first = key_index * block_rows

            def update_stats(carry, k_first=k_first):
                old_max, old_sum = carry
                scores = tile_scores(k_first)
                new_max = jnp.maximum(old_max, jnp.max(scores, axis=-1, keepdims=True))
                new_sum = old_sum * jnp.exp(old_max - new_max) + jnp.sum(
                    jnp.exp(scores - new_max), axis=-1, keepdims=True
                )
                return (new_max, new_sum)

            running_max, running_sum = lax.cond(
                live_tiles[key_index], update_stats, lambda carry: carry, (running_max, running_sum)
            )
        tiles = []
        outputs = jnp.zeros((local_heads, group_size, block_rows, HD), jnp.float32)
        for key_index in range(query_index + 1):
            k_first = key_index * block_rows

            def make_tile(accumulated, k_first=k_first):
                attention = jnp.exp(tile_scores(k_first) - running_max) / running_sum
                attention_low = attention.astype(jnp.bfloat16)
                value_block = value_all[k_first : k_first + block_rows]
                added = accumulated + jnp.einsum(
                    "gjqk,kgd->gjqd", attention_low, value_block, preferred_element_type=jnp.float32
                )
                return (attention, added)

            def skip_tile(accumulated):
                return (jnp.zeros(tile_shape, jnp.float32), accumulated)

            attention, outputs = lax.cond(live_tiles[key_index], make_tile, skip_tile, outputs)
            tiles.append(attention)
        row_delta = jnp.sum(grad_block.astype(jnp.float32) * outputs, axis=-1, keepdims=True)
        query_total = jnp.zeros((block_rows, local_heads, group_size, HD), jnp.float32)
        for key_index in range(query_index + 1):
            k_first = key_index * block_rows

            def tile_grads(accumulated, k_first=k_first, attention=tiles[key_index]):
                key_block = key_all[k_first : k_first + block_rows]
                value_block = value_all[k_first : k_first + block_rows]
                attention_low = attention.astype(jnp.bfloat16)
                grad_attention = jnp.einsum(
                    "gjqd,kgd->gjqk", grad_block, value_block, preferred_element_type=jnp.float32
                )
                grad_scores = (attention * (grad_attention - row_delta)).astype(jnp.bfloat16)
                query_add = jnp.einsum(
                    "gjqk,kgd->qgjd", grad_scores, key_block, preferred_element_type=jnp.float32
                )
                key_add = jnp.einsum(
                    "gjqk,qgjd->kgd", grad_scores, query_block, preferred_element_type=jnp.float32
                )
                value_add = jnp.einsum(
                    "gjqk,gjqd->kgd", attention_low, grad_block, preferred_element_type=jnp.float32
                )
                return (accumulated + query_add, key_add, value_add)

            def no_grads(accumulated):
                empty = jnp.zeros((block_rows, local_heads, HD), jnp.float32)
                return (accumulated, empty, empty)

            query_total, key_add, value_add = lax.cond(
                live_tiles[key_index], tile_grads, no_grads, query_total
            )
            key_parts[key_index] = key_parts[key_index] + key_add
            value_parts[key_index] = value_parts[key_index] + value_add
        pieces.append((query_total * score_scale).astype(jnp.bfloat16))
    query_out = jnp.concatenate(pieces, axis=0).reshape(ROW_LEN, local_heads * group_size * HD)
    key_out = (jnp.concatenate(key_parts, axis=0) * score_scale).astype(jnp.bfloat16)
    value_out = jnp.concatenate(value_parts, axis=0).astype(jnp.bfloat16)
    stacked = jnp.stack([key_out, value_out], axis=2).reshape(ROW_LEN, local_heads * 2 * HD)
    return (query_out, stacked)


def shards(
    layer_input, query_states, key_states, value_states, output_grad, doc_lengths, send_order
):
    row_count = doc_lengths.shape[0]
    moved_count = row_count // 2
    rank_count = lax.axis_size("dp")
    far_bit = rank_count.bit_length() - 2
    segment = segment_ids(doc_lengths)
    token_total = lax.psum(jnp.sum(doc_lengths).astype(jnp.float32), "dp")
    row_order = send_order[0]

    def by_rows(array_in):
        return array_in.reshape(row_count, ROW_LEN, array_in.shape[-1])

    input_rows = by_rows(layer_input)
    query_rows = by_rows(query_states)
    key_rows = by_rows(key_states)
    value_rows = by_rows(value_states)
    grad_rows = by_rows(output_grad)
    input_sorted = jnp.take(input_rows, row_order, axis=0)
    query_sorted = jnp.take(query_rows, row_order, axis=0)
    key_sorted = jnp.take(key_rows, row_order, axis=0)
    value_sorted = jnp.take(value_rows, row_order, axis=0)
    grad_sorted = jnp.take(grad_rows, row_order, axis=0)
    segment_sorted = jnp.take(segment, row_order, axis=0).astype(jnp.bfloat16)
    arrived = partner(
        (
            input_sorted[:moved_count],
            query_sorted[:moved_count],
            key_sorted[:moved_count],
            value_sorted[:moved_count],
            grad_sorted[:moved_count],
            segment_sorted[:moved_count],
        ),
        "dp",
        far_bit,
    )
    input_local = jnp.concatenate([input_sorted[moved_count:], arrived[0]], axis=0)
    query_local = jnp.concatenate([query_sorted[moved_count:], arrived[1]], axis=0)
    key_local = jnp.concatenate([key_sorted[moved_count:], arrived[2]], axis=0)
    value_local = jnp.concatenate([value_sorted[moved_count:], arrived[3]], axis=0)
    grad_local = jnp.concatenate([grad_sorted[moved_count:], arrived[4]], axis=0)
    segment_local = jnp.concatenate([segment_sorted[moved_count:], arrived[5]], axis=0).astype(
        jnp.int32
    )
    query_out, kv_grads = lax.map(
        attend_row, (query_local, key_local, value_local, grad_local, segment_local)
    )
    query_grad = query_out.reshape(-1, query_out.shape[-1])
    input_flat = input_local.reshape(-1, input_local.shape[-1])
    kv_flat = kv_grads.reshape(-1, kv_grads.shape[-1])
    all_grads = lax.all_gather(kv_flat, "tensor", axis=1, tiled=True)
    summed = lax.psum_scatter(
        lax.dot_general(
            all_grads, input_flat, (((0,), (0,)), ((), ())), preferred_element_type=jnp.float32
        ).astype(jnp.bfloat16),
        "dp",
        scatter_dimension=0,
        tiled=True,
    ).astype(jnp.float32)
    weight_grad = summed * (loss_scale / token_total)
    return (query_grad, weight_grad)


def solution(mesh):
    placed = (
        P("dp", "tensor"),
        P("dp", "tensor"),
        P("dp", "tensor"),
        P("dp", "tensor"),
        P("dp", "tensor"),
        P("dp", None),
        P("dp", None),
    )
    return jax.shard_map(
        shards,
        mesh=mesh,
        in_specs=placed,
        out_specs=(P("dp", "tensor"), P("dp", "tensor")),
        check_vma=False,
    )
```

profile of v0, /device:TPU:8, one launch (start us, length us, event | category | flops | bytes accessed | tf_op | source)
XLA Modules:
  0.0 915.7 jit_solution(3953882771418587068)
XLA Ops:
  10.4 2.4 gather_fusion.1
  14.1 7.3 collective-permute-start.1
  22.2 2.4 gather_fusion.5
  24.6 4.4 gather_fusion.4
  28.9 2.4 gather_fusion.3
  31.4 5.9 broadcast_select_fusion
  39.0 5.9 collective-permute-start.3
  47.6 6.0 collective-permute-start
  53.6 108.0 %collective-permute-done = bf16[1,1024]{1,0:T(2,128)(2,1)S(1)} collective-permute-done((bf16[1,1024]{1,0:T(2,128)(2,1)S(1)}, bf16[1,1024]{1,0:T(2,128)(2,1)S(1)}, u32[]{:S(2)}, u32[]{:S(2)}) %collective-permute-start) | collective-permute-done | bytes 2080 | tf_op jit(solution)/shard_map/ppermute | solution.py:20
  164.6 3.2 pad_maximum_fusion.1
  167.8 3.1 pad_maximum_fusion.2
  170.9 329.1 %while.12 = (s32[]{:T(128)}, bf16[2,1024,640]{2,1,0:T(8,128)(2,1)}, bf16[2,1024,256]{2,1,0:T(8,128)(2,1)}, s32[2,1024]{1,0:T(2,128)S(1)}, bf16[2,1024,128]{2,1,0...) while((s32[]{:T(128)}, bf16[2,1024,640]{2,1,0:T(8,128)(2,1)}, ...), condition=%wide.region_299.302_spmd, body=%wide.region_2.301_spmd.sunk | while | flops 5339790848 | bytes 285247168 | solution.py:199
  177.3 2.4 constant_dynamic-slice_fusion.16
  180.3 2.3 conditional.217
  182.7 2.4 conditional.218
  191.0 2.3 conditional.221
  193.3 2.3 conditional.222
  195.9 2.6 conditional.223
  198.5 2.1 conditional.224
  207.7 2.3 conditional.229
  210.0 2.3 conditional.230
  213.3 2.6 conditional.232
  216.0 2.1 conditional.233
  325.8 2.4 constant_dynamic-slice_fusion.16
  328.8 2.3 conditional.217
  331.1 2.4 conditional.218
  339.4 2.3 conditional.221
  341.7 2.3 conditional.222
  344.3 2.6 conditional.223
  347.0 2.1 conditional.224
  356.1 2.3 conditional.229
  358.5 2.3 conditional.230
  361.8 2.6 conditional.232
  375.6 2.5 conditional.239
  378.2 2.3 conditional.240
  380.5 2.3 conditional.241
  385.8 3.3 conditional.244
  402.6 2.3 conditional.254
  404.9 2.3 conditional.255
  408.8 2.6 conditional.259
  411.4 2.7 conditional.260
  428.0 2.3 conditional.271
  430.3 2.3 conditional.272
  502.1 40.7 %collective-permute-done.5 = bf16[1,1024,640]{2,1,0:T(8,128)(2,1)S(1)} collective-permute-done((bf16[1,1024,640]{2,1,0:T(8,128)(2,1)S(1)}, bf16[1,1024,640]{2,1,0:T(8,128)(2,1)S(1)}, u32[]{:S(2)}, u32[]{:S(2)}) %collective-permute-start.5) | collective-permute-done | bytes 1310752 | tf_op jit(solution)/shard_map/ppermute | solution.py:20
  544.8 131.4 %all-gather.2.cloned.1.call-done = bf16[2048,2048]{1,0:T(8,128)(2,1)} async-done(((bf16[2048,256]{1,0:T(8,128)(2,1)}), bf16[2048,2048]{1,0:T(8,128)(2,1)}) %all-gather.2.cloned.1.call-update) | async-done | bytes 8388624 | tf_op jit(solution)/shard_map/all_gather | solution.py:205
  676.2 11.2 %convolution_convert_fusion = bf16[2048,640]{1,0:T(8,128)(2,1)} fusion(bf16[2048,2048]{1,0:T(8,128)(2,1)} %all-gather.2.cloned.1.call-done, bf16[2048,640]{1,0:T(8,128)(2,1)} %bitcast.4553), kind=kOutput, calls=%fused_computation.1657 | convolution fusion | flops 5370019840 | bytes 13631488 | tf_op jit(solution)/shard_map/dot_general | solution.py:207
  689.4 75.6 %psum.7 = f32[]{:T(128)} all-reduce(f32[]{:T(128)S(6)} %convert_element_type.712), channel_id=1, replica_groups=mesh['dp'=32,'tensor'=8] {'dp'}, use_global_device_ids=true, to_apply=%region_302.305 | all-reduce | flops 1 | bytes 8 | tf_op jit(solution)/shard_map/psum | solution.py:162
  765.7 141.1 %reduce-scatter.2.cloned.1.call-done = bf16[64,640]{1,0:T(8,128)(2,1)} async-done(((bf16[2048,640]{1,0:T(8,128)(2,1)}), bf16[64,640]{1,0:T(8,128)(2,1)}) %reduce-scatter.2.cloned.1.call-update) | async-done | bytes 81936 | tf_op jit(solution)/shard_map/reduce_scatter | solution.py:206
  (1470 shorter events, 298.6 us)
Async XLA Ops:
  7.2 15.1 %copy-start = (bf16[2048,640]{1,0:T(8,128)(2,1)S(1)}, bf16[2048,640]{1,0:T(8,128)(2,1)}, u32[]{:S(2)}) copy-start(bf16[2048,640]{1,0:T(8,128)(2,1)} %param.229) | copy-start | bytes 7864324
  7.2 669.0 %all-gather.2.cloned.1.call-start = ((), (), s32[]{:S(2)}) async-start(), calls=%async_computation.1 | async-start | bytes 9437184 | tf_op jit(solution)/shard_map/all_gather | solution.py:205
  14.1 147.5 %collective-permute-start.1 = (bf16[1,1024,128]{2,1,0:T(8,128)(2,1)S(1)}, bf16[1,1024,128]{2,1,0:T(8,128)(2,1)}, u32[]{:S(2)}, u32[]{:S(2)}) collective-permute-start(bf16[1,1024,128]{2,1,0:T(8,128)(2,1)S(1)} %get-tuple-element.6064), channel_id=1, source_target_pairs={{0,128},{8,136},{16,144},{24,152},{32,160},{40,168},{48,176},{56,1... | collective-permute-start | bytes 786440 | tf_op jit(solution)/shard_map/ppermute | solution.py:20
  22.2 140.5 %collective-permute-start.2 = (bf16[1,1024,128]{2,1,0:T(8,128)(2,1)}, bf16[1,1024,128]{2,1,0:T(8,128)(2,1)}, u32[]{:S(2)}, u32[]{:S(2)}) collective-permute-start(bf16[1,1024,128]{2,1,0:T(8,128)(2,1)} %get-tuple-element.6062), channel_id=1, source_target_pairs={{0,128},{8,136},{16,144},{24,152},{32,160},{40,168},{48,176},{56,1... | collective-permute-start | bytes 786440 | tf_op jit(solution)/shard_map/ppermute | solution.py:20
  39.0 125.5 %collective-permute-start.3 = (bf16[1,1024,640]{2,1,0:T(8,128)(2,1)}, bf16[1,1024,640]{2,1,0:T(8,128)(2,1)}, u32[]{:S(2)}, u32[]{:S(2)}) collective-permute-start(bf16[1,1024,640]{2,1,0:T(8,128)(2,1)} %get-tuple-element.6060), channel_id=1, source_target_pairs={{0,128},{8,136},{16,144},{24,152},{32,160},{40,168},{48,176},{56,1... | collective-permute-start | bytes 3932168 | tf_op jit(solution)/shard_map/ppermute | solution.py:20
  46.7 117.9 %copy-start.95 = (bf16[1,1024,640]{2,1,0:T(8,128)(2,1)S(1)}, bf16[1,1024,640]{2,1,0:T(8,128)(2,1)}, u32[]{:S(2)}) copy-start(bf16[1,1024,640]{2,1,0:T(8,128)(2,1)} %get-tuple-element.6059) | copy-start | bytes 3932164
  46.7 121.2 %collective-permute-start.4 = (bf16[1,1024,640]{2,1,0:T(8,128)(2,1)}, bf16[1,1024,640]{2,1,0:T(8,128)(2,1)}, u32[]{:S(2)}, u32[]{:S(2)}) collective-permute-start(bf16[1,1024,640]{2,1,0:T(8,128)(2,1)} %get-tuple-element.6058), channel_id=1, source_target_pairs={{0,128},{8,136},{16,144},{24,152},{32,160},{40,168},{48,176},{56,1... | collective-permute-start | bytes 3932168 | tf_op jit(solution)/shard_map/ppermute | solution.py:20
  47.6 114.0 %collective-permute-start = (bf16[1,1024]{1,0:T(2,128)(2,1)S(1)}, bf16[1,1024]{1,0:T(2,128)(2,1)S(1)}, u32[]{:S(2)}, u32[]{:S(2)}) collective-permute-start(bf16[1,1024]{1,0:T(2,128)(2,1)S(1)} %get-tuple-element.6066), channel_id=1, source_target_pairs={{0,128},{8,136},{16,144},{24,152},{32,160},{40,168},{48,176},{56,1... | collective-permute-start | bytes 6152 | tf_op jit(solution)/shard_map/ppermute | solution.py:20
  215.9 8.8 copy-start.5
  230.8 8.1 copy-start.21
  230.8 8.1 copy-start.70
  245.0 10.0 %copy-start.27 = (f32[128,1,128]{2,0,1:T(8,128)}, f32[128,1,128]{2,0,1:T(8,128)S(1)}, u32[]{:S(2)}) copy-start(f32[128,1,128]{2,0,1:T(8,128)S(1)} %get-tuple-element.6682) | copy-start | bytes 196612 | tf_op jit(solution)/shard_map/while
  245.0 9.8 %copy-start.3 = (bf16[1,128,640]{2,1,0:T(8,128)(2,1)S(1)}, bf16[1,128,640]{2,1,0:T(8,128)(2,1)}, u32[]{:S(2)}) copy-start(bf16[1,128,640]{2,1,0:T(8,128)(2,1)} %get-tuple-element.6507) | copy-start | bytes 491524 | tf_op jit(solution)/shard_map/while
  245.7 9.4 %copy-start.29 = (f32[128,1,128]{2,0,1:T(8,128)}, f32[128,1,128]{2,0,1:T(8,128)S(1)}, u32[]{:S(2)}) copy-start(f32[128,1,128]{2,0,1:T(8,128)S(1)} %get-tuple-element.6685) | copy-start | bytes 196612 | tf_op jit(solution)/shard_map/while
  262.3 10.6 %copy-start.36 = (f32[128,1,128]{2,0,1:T(8,128)}, f32[128,1,128]{2,0,1:T(8,128)S(1)}, u32[]{:S(2)}) copy-start(f32[128,1,128]{2,0,1:T(8,128)S(1)} %get-tuple-element.6686) | copy-start | bytes 196612 | tf_op jit(solution)/shard_map/while
  262.3 10.4 %copy-start.2 = (bf16[1,128,640]{2,1,0:T(8,128)(2,1)S(1)}, bf16[1,128,640]{2,1,0:T(8,128)(2,1)}, u32[]{:S(2)}) copy-start(bf16[1,128,640]{2,1,0:T(8,128)(2,1)} %get-tuple-element.6541) | copy-start | bytes 491524 | tf_op jit(solution)/shard_map/while
  262.9 10.1 %copy-start.38 = (f32[128,1,128]{2,0,1:T(8,128)}, f32[128,1,128]{2,0,1:T(8,128)S(1)}, u32[]{:S(2)}) copy-start(f32[128,1,128]{2,0,1:T(8,128)S(1)} %get-tuple-element.6688) | copy-start | bytes 196612 | tf_op jit(solution)/shard_map/while
  281.0 11.4 %copy-start.47 = (f32[128,1,128]{2,0,1:T(8,128)}, f32[128,1,128]{2,0,1:T(8,128)S(1)}, u32[]{:S(2)}) copy-start(f32[128,1,128]{2,0,1:T(8,128)S(1)} %get-tuple-element.6689) | copy-start | bytes 196612 | tf_op jit(solution)/shard_map/while
  281.1 11.4 %copy-start.49 = (f32[128,1,128]{2,0,1:T(8,128)}, f32[128,1,128]{2,0,1:T(8,128)S(1)}, u32[]{:S(2)}) copy-start(f32[128,1,128]{2,0,1:T(8,128)S(1)} %get-tuple-element.6690) | copy-start | bytes 196612 | tf_op jit(solution)/shard_map/while
  281.1 11.4 %copy-start.51 = (f32[128,1,128]{0,2,1:T(8,128)}, f32[128,1,128]{0,2,1:T(8,128)S(1)}, u32[]{:S(2)}) copy-start(f32[128,1,128]{0,2,1:T(8,128)S(1)} %get-tuple-element.6654) | copy-start | bytes 196612 | tf_op jit(solution)/shard_map/while
  306.1 9.0 copy-start.55
  306.1 9.1 copy-start.42
  306.1 9.2 %copy-start.33 = (f32[128,1,128]{2,0,1:T(8,128)S(1)}, f32[128,1,128]{2,0,1:T(8,128)}, u32[]{:S(2)}) copy-start(f32[128,1,128]{2,0,1:T(8,128)} %copy-done.32) | copy-start | bytes 196612 | tf_op jit(solution)/shard_map/while
  306.2 9.2 %copy-start.26 = (f32[128,1,128]{2,0,1:T(8,128)S(1)}, f32[128,1,128]{2,0,1:T(8,128)}, u32[]{:S(2)}) copy-start(f32[128,1,128]{2,0,1:T(8,128)} %copy-done.25) | copy-start | bytes 196612 | tf_op jit(solution)/shard_map/while
  306.2 9.3 %copy-start.18 = (f32[128,1,128]{2,0,1:T(8,128)S(1)}, f32[128,1,128]{2,0,1:T(8,128)}, u32[]{:S(2)}) copy-start(f32[128,1,128]{2,0,1:T(8,128)} %copy-done.17) | copy-start | bytes 196612 | tf_op jit(solution)/shard_map/while
  308.1 8.5 copy-start.57
  308.1 8.6 copy-start.44
  364.4 8.8 copy-start.5
  389.1 9.9 %copy-start.4 = (bf16[1,128,640]{2,1,0:T(8,128)(2,1)S(1)}, bf16[1,128,640]{2,1,0:T(8,128)(2,1)}, u32[]{:S(2)}) copy-start(bf16[1,128,640]{2,1,0:T(8,128)(2,1)} %get-tuple-element.6478) | copy-start | bytes 491524 | tf_op jit(solution)/shard_map/while
  411.4 12.0 %copy-start.27 = (f32[128,1,128]{2,0,1:T(8,128)}, f32[128,1,128]{2,0,1:T(8,128)S(1)}, u32[]{:S(2)}) copy-start(f32[128,1,128]{2,0,1:T(8,128)S(1)} %get-tuple-element.6682) | copy-start | bytes 196612 | tf_op jit(solution)/shard_map/while
  411.4 11.8 %copy-start.3 = (bf16[1,128,640]{2,1,0:T(8,128)(2,1)S(1)}, bf16[1,128,640]{2,1,0:T(8,128)(2,1)}, u32[]{:S(2)}) copy-start(bf16[1,128,640]{2,1,0:T(8,128)(2,1)} %get-tuple-element.6507) | copy-start | bytes 491524 | tf_op jit(solution)/shard_map/while
  414.1 9.4 %copy-start.29 = (f32[128,1,128]{2,0,1:T(8,128)}, f32[128,1,128]{2,0,1:T(8,128)S(1)}, u32[]{:S(2)}) copy-start(f32[128,1,128]{2,0,1:T(8,128)S(1)} %get-tuple-element.6685) | copy-start | bytes 196612 | tf_op jit(solution)/shard_map/while
  437.0 12.6 %copy-start.36 = (f32[128,1,128]{2,0,1:T(8,128)}, f32[128,1,128]{2,0,1:T(8,128)S(1)}, u32[]{:S(2)}) copy-start(f32[128,1,128]{2,0,1:T(8,128)S(1)} %get-tuple-element.6686) | copy-start | bytes 196612 | tf_op jit(solution)/shard_map/while
  437.0 12.4 %copy-start.2 = (bf16[1,128,640]{2,1,0:T(8,128)(2,1)S(1)}, bf16[1,128,640]{2,1,0:T(8,128)(2,1)}, u32[]{:S(2)}) copy-start(bf16[1,128,640]{2,1,0:T(8,128)(2,1)} %get-tuple-element.6541) | copy-start | bytes 491524 | tf_op jit(solution)/shard_map/while
  439.6 10.1 %copy-start.38 = (f32[128,1,128]{2,0,1:T(8,128)}, f32[128,1,128]{2,0,1:T(8,128)S(1)}, u32[]{:S(2)}) copy-start(f32[128,1,128]{2,0,1:T(8,128)S(1)} %get-tuple-element.6688) | copy-start | bytes 196612 | tf_op jit(solution)/shard_map/while
  457.6 11.4 %copy-start.47 = (f32[128,1,128]{2,0,1:T(8,128)}, f32[128,1,128]{2,0,1:T(8,128)S(1)}, u32[]{:S(2)}) copy-start(f32[128,1,128]{2,0,1:T(8,128)S(1)} %get-tuple-element.6689) | copy-start | bytes 196612 | tf_op jit(solution)/shard_map/while
  457.7 11.4 %copy-start.49 = (f32[128,1,128]{2,0,1:T(8,128)}, f32[128,1,128]{2,0,1:T(8,128)S(1)}, u32[]{:S(2)}) copy-start(f32[128,1,128]{2,0,1:T(8,128)S(1)} %get-tuple-element.6690) | copy-start | bytes 196612 | tf_op jit(solution)/shard_map/while
  457.7 11.4 %copy-start.51 = (f32[128,1,128]{0,2,1:T(8,128)}, f32[128,1,128]{0,2,1:T(8,128)S(1)}, u32[]{:S(2)}) copy-start(f32[128,1,128]{0,2,1:T(8,128)S(1)} %get-tuple-element.6654) | copy-start | bytes 196612 | tf_op jit(solution)/shard_map/while
  482.6 9.0 copy-start.55
  482.6 9.1 copy-start.42
  482.6 9.2 %copy-start.33 = (f32[128,1,128]{2,0,1:T(8,128)S(1)}, f32[128,1,128]{2,0,1:T(8,128)}, u32[]{:S(2)}) copy-start(f32[128,1,128]{2,0,1:T(8,128)} %copy-done.32) | copy-start | bytes 196612 | tf_op jit(solution)/shard_map/while
  482.6 9.2 %copy-start.26 = (f32[128,1,128]{2,0,1:T(8,128)S(1)}, f32[128,1,128]{2,0,1:T(8,128)}, u32[]{:S(2)}) copy-start(f32[128,1,128]{2,0,1:T(8,128)} %copy-done.25) | copy-start | bytes 196612 | tf_op jit(solution)/shard_map/while
  482.7 9.3 %copy-start.18 = (f32[128,1,128]{2,0,1:T(8,128)S(1)}, f32[128,1,128]{2,0,1:T(8,128)}, u32[]{:S(2)}) copy-start(f32[128,1,128]{2,0,1:T(8,128)} %copy-done.17) | copy-start | bytes 196612 | tf_op jit(solution)/shard_map/while
  484.5 8.5 copy-start.57
  484.6 8.6 copy-start.44
  500.1 406.8 %reduce-scatter.2.cloned.1.call-start = ((), (), s32[]{:S(2)}) async-start(), calls=%async_computation.2 | async-start | bytes 2703360 | tf_op jit(solution)/shard_map/reduce_scatter | solution.py:206
  502.0 40.8 %collective-permute-start.5 = (bf16[1,1024,640]{2,1,0:T(8,128)(2,1)S(1)}, bf16[1,1024,640]{2,1,0:T(8,128)(2,1)S(1)}, u32[]{:S(2)}, u32[]{:S(2)}) collective-permute-start(bf16[1,1024,640]{2,1,0:T(8,128)(2,1)S(1)} %get-tuple-element.6056), channel_id=1, source_target_pairs={{0,128},{8,136},{16,144},{24,152},{32,160},{40,168},{48,176},{56,1... | collective-permute-start | bytes 3932168 | tf_op jit(solution)/shard_map/ppermute | solution.py:20
  676.2 232.2 %copy-start.1 = (bf16[2048,640]{1,0:T(8,128)(2,1)S(1)}, bf16[2048,640]{1,0:T(8,128)(2,1)}, u32[]{:S(2)}) copy-start(bf16[2048,640]{1,0:T(8,128)(2,1)} %param.229) | copy-start | bytes 7864324
  (154 other events, 504.3 us)
Sparse Core Ops, SparseCore 0:
  500.2 175.9 all-gather.1
  687.6 219.2 reduce-scatter.1
where the time goes:
time: 929 us; the launch traced here: 916 us
  waiting for transfers between devices  421 us (45%)
  local copies, waits for them, and re-layouts  151 us (16%)
  loops' own time  115 us (12%)
  blocking collectives  75.6 us (8%)
  matrix products  71.3 us (8%)
  other arithmetic  46.1 us (5%)
  starting transfers between devices  19.4 us (2%)
  between operations  16 us (2%)
    ppermute x6, waiting for transfers between devices, partner(): return lax.ppermute(value, axis, pairs)  149 us
    reduce_scatter x1, waiting for transfers between devices, shards(): lax.psum_scatter(lax.dot_general(all_grads, input_flat, (((0,), (0,)), ((...  141 us
    all_gather x1, waiting for transfers between devices, shards(): all_grads = lax.all_gather(kv_flat, 'tensor', axis=1, tiled=True)  131 us
    another operation x1, loops' own time, shards(): lax.map(attend_row, (query_local, key_local, value_local, grad_local, seg...  108 us
    psum x1, blocking collectives, shards(): token_total = lax.psum(jnp.sum(doc_lengths).astype(jnp.float32), 'dp')  75.6 us
    another operation x226, local copies, waits for them, and re-layouts  64.6 us
    while x388, local copies, waits for them, and re-layouts  21.9 us
    dot_general x17, matrix products, make_tile(): jnp.einsum('gjqk,kgd->gjqd', attention_low, value_block, preferred_elemen...  20.6 us
  transfers between devices with their start and end apart: 8, of which 4 were waited for; matrix products, arithmetic and copies ran while one was open for 3% of the time, Pallas kernels for 0%

commit v1 on v0

v1 whole, which is shorter than its diff:
```python
import functools
import math

import jax
import jax.numpy as jnp
from jax import lax
from jax.experimental import pallas as pl
from jax.experimental.pallas import tpu as pltpu
from jax.sharding import PartitionSpec as P

QH = 40
KVH = 8
HD = 128
ROW_LEN = 1024
DOCS = 8
GROUP = QH // KVH
BQ = 256

loss_scale = 256.0
masked_score = -1e30
score_scale = HD ** (-0.5)
exp_scale = score_scale * math.log2(math.e)


def attend_block(qb, head, q_ref, g_ref, k_ref, v_ref, kt_ref, start, live, dq_ref, dk_ref, dv_ref):
    q_first = qb * BQ
    length = q_first + BQ
    lanes = pl.ds(pl.multiple_of(head * HD, HD), HD)
    query = q_ref[q_first:length, lanes]
    grad = g_ref[q_first:length, lanes]
    scores = lax.dot_general(
        k_ref[:length, :], query, (((1,), (1,)), ((), ())), preferred_element_type=jnp.float32
    )
    key_index = lax.broadcasted_iota(jnp.int32, (length, BQ), 0)
    query_index = lax.broadcasted_iota(jnp.int32, (1, BQ), 1) + q_first
    allowed = (key_index >= start) & (key_index <= query_index)
    scores = jnp.where(allowed, scores, masked_score)
    top = jnp.max(scores, axis=0, keepdims=True)
    exponent = jnp.exp2((scores - top) * exp_scale)
    total = jnp.sum(exponent, axis=0, keepdims=True)
    grad_probs = lax.dot_general(
        v_ref[:length, :], grad, (((1,), (1,)), ((), ())), preferred_element_type=jnp.float32
    )
    weighted = jnp.sum(exponent * grad_probs, axis=0, keepdims=True)
    inverse = live / total
    delta = weighted / total
    probs = exponent * inverse
    probs_low = probs.astype(jnp.bfloat16)
    grad_scores = (probs * (grad_probs - delta)).astype(jnp.bfloat16)
    dv_ref[:length, :] += jnp.dot(probs_low, grad, preferred_element_type=jnp.float32)
    dk_ref[:length, :] += jnp.dot(grad_scores, query, preferred_element_type=jnp.float32)
    dq_t = jnp.dot(kt_ref[:, :length], grad_scores, preferred_element_type=jnp.float32)
    dq_ref[q_first:length, lanes] = (dq_t.T * score_scale).astype(jnp.bfloat16)


def attention_kernel(
    order_ref, q_ref, k_ref, v_ref, g_ref, start_ref, live_ref, dq_ref, kv_ref, kt_ref, dk_ref, dv_ref
):
    kt_ref[...] = k_ref[0].astype(jnp.float32).T.astype(jnp.bfloat16)
    dk_ref[...] = jnp.zeros_like(dk_ref)
    dv_ref[...] = jnp.zeros_like(dv_ref)

    @pl.loop(0, GROUP)
    def _(head):
        for qb in range(ROW_LEN // BQ):
            columns = slice(qb * BQ, qb * BQ + BQ)
            attend_block(
                qb,
                head,
                q_ref.at[0],
                g_ref.at[0],
                k_ref.at[0],
                v_ref.at[0],
                kt_ref,
                start_ref[0, :, columns],
                live_ref[0, :, columns],
                dq_ref.at[0],
                dk_ref,
                dv_ref,
            )

    kv_ref[0, :, :HD] = (dk_ref[...] * score_scale).astype(jnp.bfloat16)
    kv_ref[0, :, HD:] = dv_ref[...].astype(jnp.bfloat16)


def attention(order, query, key, value, grad, start, live):
    rows = query.shape[0]

    def picked(i, order_ref):
        return (order_ref[i], 0, 0)

    def block(width):
        return pl.BlockSpec((1, ROW_LEN, width), picked)

    return pl.pallas_call(
        attention_kernel,
        out_shape=(
            jax.ShapeDtypeStruct((rows, ROW_LEN, GROUP * HD), jnp.bfloat16),
            jax.ShapeDtypeStruct((rows, ROW_LEN, 2 * HD), jnp.bfloat16),
        ),
        grid_spec=pltpu.PrefetchScalarGridSpec(
            num_scalar_prefetch=1,
            grid=(rows,),
            in_specs=[
                block(GROUP * HD),
                block(HD),
                block(HD),
                block(GROUP * HD),
                pl.BlockSpec((1, 1, ROW_LEN), picked),
                pl.BlockSpec((1, 1, ROW_LEN), picked),
            ],
            out_specs=[
                pl.BlockSpec((1, ROW_LEN, GROUP * HD), lambda i, order_ref: (i, 0, 0)),
                pl.BlockSpec((1, ROW_LEN, 2 * HD), picked),
            ],
            scratch_shapes=[
                pltpu.VMEM((HD, ROW_LEN), jnp.bfloat16),
                pltpu.VMEM((ROW_LEN, HD), jnp.float32),
                pltpu.VMEM((ROW_LEN, HD), jnp.float32),
            ],
        ),
        compiler_params=pltpu.CompilerParams(vmem_limit_bytes=48 << 20),
        name="attention_backward",
    )(order, query, key, value, grad, start, live)


def document_starts(doc_lengths):
    ends = jnp.cumsum(doc_lengths, axis=1)
    position = jnp.arange(ROW_LEN, dtype=jnp.int32)
    passed = position[None, :, None] >= ends[:, None, :]
    start = jnp.max(jnp.where(passed, ends[:, None, :], 0), axis=2)
    live = (position[None, :] < ends[:, -1:]).astype(jnp.float32)
    return start[:, None, :], live[:, None, :]


def shards(
    layer_input, query_states, key_states, value_states, output_grad, doc_lengths, send_order
):
    rows = doc_lengths.shape[0]
    ranks = lax.axis_size("dp")
    half = ranks // 2
    start, live = document_starts(doc_lengths)
    token_total = lax.psum(jnp.sum(doc_lengths).astype(jnp.float32), "dp")

    def by_rows(array_in):
        return array_in.reshape(rows, ROW_LEN, array_in.shape[-1])

    dq, kv = attention(
        send_order[0],
        by_rows(query_states),
        by_rows(key_states),
        by_rows(value_states),
        by_rows(output_grad),
        start,
        live,
    )
    arrived = lax.ppermute(dq[:1], "dp", [(r, (r + half) % ranks) for r in range(ranks)])
    query_grad = jnp.concatenate([dq[1:], arrived], axis=0).reshape(-1, dq.shape[-1])
    all_kv = lax.all_gather(kv.reshape(-1, 2 * HD), "tensor", axis=1, tiled=True)
    partial = lax.dot_general(
        all_kv, layer_input, (((0,), (0,)), ((), ())), preferred_element_type=jnp.float32
    ).astype(jnp.bfloat16)
    summed = lax.psum_scatter(partial, "dp", scatter_dimension=0, tiled=True)
    weight_grad = summed.astype(jnp.float32) * (loss_scale / token_total)
    return (query_grad, weight_grad)


def solution(mesh):
    placed = (P("dp", "tensor"),) * 5 + (P("dp", None),) * 2
    return jax.shard_map(
        shards,
        mesh=mesh,
        in_specs=placed,
        out_specs=(P("dp", "tensor"), P("dp", "tensor")),
        check_vma=False,
    )
```

time: 929 us -> 384 us (0.41)
  the two profiles are of different devices: /device:TPU:8 before, /device:TPU:25 now
where the time goes in v1:
time: 384 us; the launch traced here: 378 us
  waiting for transfers between devices  188 us (49%)
  blocking collectives  107 us (28%)
  Pallas kernels  36 us (9%)
  between operations  15.4 us (4%)
  matrix products  10.3 us (3%)
  local copies, waits for them, and re-layouts  8.94 us (2%)
  other arithmetic  6.9 us (2%)
  starting transfers between devices  5.58 us (1%)
    reduce_scatter x1, waiting for transfers between devices, shards(): summed = lax.psum_scatter(partial, 'dp', scatter_dimension=0, tiled=True)  129 us
    psum x1, blocking collectives, shards(): token_total = lax.psum(jnp.sum(doc_lengths).astype(jnp.float32), 'dp')  107 us
    all_gather x1, waiting for transfers between devices, shards(): lax.all_gather(kv.reshape(-1, 2 * HD), 'tensor', axis=1, tiled=True)  59 us
    pallas_call x1, Pallas kernels, attention(): pl.pallas_call(attention_kernel, out_shape=(jax.ShapeDtypeStruct((rows, R...  36 us
    dot_general x1, matrix products, shards(): lax.dot_general(all_kv, layer_input, (((0,), (0,)), ((), ())), preferred_...  10.3 us
  transfers between devices with their start and end apart: 3, of which 2 were waited for; matrix products, arithmetic and copies ran while one was open for 2% of the time, Pallas kernels for 0%

profile of v1, /device:TPU:25, one launch (start us, length us, event | category | flops | bytes accessed | tf_op | source)
XLA Modules:
  0.0 378.2 jit_solution(10411683533620324309)
XLA Ops:
  7.2 0.0 copy-start
  7.2 0.0 all-gather.2.cloned.1.call-start
  7.2 1.0 reduce_window_sum.11
  8.2 0.1 select_reduce_fusion
  8.3 0.2 slice_reduce_fusion
  8.5 0.1 compare_convert_fusion.live_ref
  8.6 0.0 copy-start.3
  8.6 1.0 copy-done.3
  9.7 0.0 copy-start.4
  9.7 1.0 copy-done.4
  10.7 0.0 copy-start.5
  10.7 0.7 copy-done.5
  11.3 36.0 %attention_backward.1 = (bf16[2,1024,640]{2,1,0:T(8,128)(2,1)S(1)}, bf16[2,1024,256]{2,1,0:T(8,128)(2,1)S(1)}) custom-call(s32[2]{0:T(128)S(1)} %bitcast.12, bf16[2,1024,640]{2,1,0:T(8,128)(2,1)} %bitcast.13, bf16[2,1024,128]{2,1,0:T(8,128)(2,1)S(1)} %bitcast.10, bf16[2,1024,128]{2,1,0:T(8,128)(2,1)S(1)} %bitcast.11, bf16[2,1024,640]{2,1,0:T(8,128)(2,1)} %bitcast.14, ...), custom_call_target="tpu_custom_call" | custom-call | tf_op jit(solution)/shard_map/attention_backward/pallas_call | solution.py:95
  47.3 0.0 copy-start.1
  47.4 1.5 copy-done.1
  48.8 0.0 copy-start.2
  48.8 1.1 copy-done.2
  49.9 0.0 all-gather.2.cloned.1.call-update
  49.9 0.0 reduce-scatter.2.cloned.1.call-start
  50.0 59.0 %all-gather.2.cloned.1.call-done = bf16[2048,2048]{1,0:T(8,128)(2,1)} async-done(((bf16[2048,256]{1,0:T(8,128)(2,1)}), bf16[2048,2048]{1,0:T(8,128)(2,1)}) %all-gather.2.cloned.1.call-update) | async-done | bytes 8388624 | tf_op jit(solution)/shard_map/all_gather | solution.py:159
  109.0 0.0 copy-done
  109.0 10.3 %convolution_convert_fusion = bf16[2048,640]{1,0:T(8,128)(2,1)} fusion(bf16[2048,2048]{1,0:T(8,128)(2,1)} %all-gather.2.cloned.1.call-done, bf16[2048,640]{1,0:T(8,128)(2,1)S(1)} %copy-done), kind=kOutput, calls=%fused_computation | convolution fusion | flops 5370019840 | bytes 13631488 | tf_op jit(solution)/shard_map/dot_general | solution.py:160
  119.3 0.0 reduce-scatter.2.cloned.1.call-update
  119.3 0.0 copy-start.6
  119.3 3.4 fusion
  122.7 5.5 %collective-permute-start = (bf16[1,1024,640]{2,1,0:T(8,128)(2,1)}, bf16[1,1024,640]{2,1,0:T(8,128)(2,1)}, u32[]{:S(2)}, u32[]{:S(2)}) collective-permute-start(bf16[1,1024,640]{2,1,0:T(8,128)(2,1)} %get-tuple-element.7), channel_id=1, source_target_pairs={{0,128},{8,136},{16,144},{24,152},{32,160},{40,168},{48,176},{56,1... | collective-permute-start | bytes 3932168 | tf_op jit(solution)/shard_map/ppermute | solution.py:157
  128.2 0.0 copy-done.6
  128.2 0.6 reduce_sum.9
  129.5 106.7 %psum.7 = f32[]{:T(128)} all-reduce(f32[]{:T(128)S(6)} %convert_element_type.22), channel_id=1, replica_groups=mesh['dp'=32,'tensor'=8] {'dp'}, use_global_device_ids=true, to_apply=%region_4.5 | all-reduce | flops 1 | bytes 8 | tf_op jit(solution)/shard_map/psum | solution.py:143
  237.0 0.0 collective-permute-done
  237.0 3.5 pad_maximum_fusion
  240.5 129.3 %reduce-scatter.2.cloned.1.call-done = bf16[64,640]{1,0:T(8,128)(2,1)} async-done(((bf16[2048,640]{1,0:T(8,128)(2,1)}), bf16[64,640]{1,0:T(8,128)(2,1)}) %reduce-scatter.2.cloned.1.call-update) | async-done | bytes 81936 | tf_op jit(solution)/shard_map/reduce_scatter | solution.py:163
  369.8 1.6 convert_multiply_fusion
  (1 shorter events, 0.0 us)
Async XLA Ops:
  7.2 101.8 %copy-start = (bf16[2048,640]{1,0:T(8,128)(2,1)S(1)}, bf16[2048,640]{1,0:T(8,128)(2,1)}, u32[]{:S(2)}) copy-start(bf16[2048,640]{1,0:T(8,128)(2,1)} %param.7) | copy-start | bytes 7864324
  7.2 101.8 %all-gather.2.cloned.1.call-start = ((), (), s32[]{:S(2)}) async-start(), calls=%async_computation.1 | async-start | bytes 9437184 | tf_op jit(solution)/shard_map/all_gather | solution.py:159
  8.6 1.0 copy-start.3
  9.7 1.0 copy-start.4
  10.7 0.7 copy-start.5
  47.3 1.5 copy-start.1
  48.8 1.1 copy-start.2
  49.9 319.8 %reduce-scatter.2.cloned.1.call-start = ((), (), s32[]{:S(2)}) async-start(), calls=%async_computation.2 | async-start | bytes 2703360 | tf_op jit(solution)/shard_map/reduce_scatter | solution.py:163
  119.3 9.0 %copy-start.6 = (s32[2,8]{1,0:T(2,128)S(1)}, s32[2,8]{1,0:T(2,128)}, u32[]{:S(2)}) copy-start(s32[2,8]{1,0:T(2,128)} %param.12) | copy-start | bytes 196
  122.7 114.2 %collective-permute-start = (bf16[1,1024,640]{2,1,0:T(8,128)(2,1)}, bf16[1,1024,640]{2,1,0:T(8,128)(2,1)}, u32[]{:S(2)}, u32[]{:S(2)}) collective-permute-start(bf16[1,1024,640]{2,1,0:T(8,128)(2,1)} %get-tuple-element.7), channel_id=1, source_target_pairs={{0,128},{8,136},{16,144},{24,152},{32,160},{40,168},{48,176},{56,1... | collective-permute-start | bytes 3932168 | tf_op jit(solution)/shard_map/ppermute | solution.py:157
Sparse Core Ops, SparseCore 0:
  50.1 58.8 all-gather.1
  119.4 250.3 reduce-scatter.1

commit v2 on v1

v2 whole, which is shorter than its diff:
```python
import math

import jax
import jax.numpy as jnp
from jax import lax
from jax.experimental import pallas as pl
from jax.experimental.pallas import tpu as pltpu
from jax.sharding import PartitionSpec as P

QH = 40
KVH = 8
HD = 128
ROW_LEN = 1024
DOCS = 8
GROUP = QH // KVH
BQ = 256
BLOCKS = ROW_LEN // BQ
ROWS = 2
NX, NY, NZ = 4, 4, 8
NT = 8
WIDTH = GROUP * HD
FEATURES = 2 * HD
PART = FEATURES // NX
HALF = PART // 2
LAG_B = 2
LAG_C = 4

loss_scale = 256.0
masked_score = -1e30
score_scale = HD ** (-0.5)
exp_scale = score_scale * math.log2(math.e)
MESH = pl.DeviceIdType.MESH
f32 = jnp.float32
bf16 = jnp.bfloat16


def attend_block(qb, query, grad, k_ref, v_ref, kt_ref, row, ends, dk_ref, dv_ref):
    q_first = qb * BQ
    length = q_first + BQ
    scores = lax.dot_general(
        k_ref[row, :length, :], query, (((1,), (1,)), ((), ())), preferred_element_type=f32
    )
    query_index = lax.broadcasted_iota(jnp.int32, (1, BQ), 1) + q_first
    start = jnp.zeros((1, BQ), jnp.int32)
    for end in ends:
        start = jnp.where(query_index >= end, end, start)
    live = jnp.where(query_index < ends[-1], 1.0, 0.0).astype(f32)
    key_index = lax.broadcasted_iota(jnp.int32, (length, BQ), 0)
    allowed = (key_index >= start) & (key_index <= query_index)
    scores = jnp.where(allowed, scores, masked_score)
    top = jnp.max(scores, axis=0, keepdims=True)
    exponent = jnp.exp2((scores - top) * exp_scale)
    total = jnp.sum(exponent, axis=0, keepdims=True)
    grad_probs = lax.dot_general(
        v_ref[row, :length, :], grad, (((1,), (1,)), ((), ())), preferred_element_type=f32
    )
    weighted = jnp.sum(exponent * grad_probs, axis=0, keepdims=True)
    inverse = live / total
    delta = weighted / total
    probs = exponent * inverse
    probs_low = probs.astype(bf16)
    grad_scores = (probs * (grad_probs - delta)).astype(bf16)
    dv_ref[:length, :] += jnp.dot(probs_low, grad, preferred_element_type=f32)
    dk_ref[:length, :] += jnp.dot(grad_scores, query, preferred_element_type=f32)
    dq_t = jnp.dot(kt_ref[:, :length], grad_scores, preferred_element_type=f32)
    return (dq_t.T * score_scale).astype(bf16)


def whole_kernel(
    order_ref, lengths_ref, x_hbm, q_hbm, k_hbm, v_hbm, g_hbm,
    dq_hbm, w_ref,
    x_ref, q_ref, k_ref, v_ref, g_ref, kt_ref, dk_ref, dv_ref, dq_ref, kv_ref, wt_ref,
    s1_ref, r1_ref, s2_ref, r2_ref, zs_ref, zr_ref, count_ref, cx_ref, plane_ref, cz_ref,
    in_sem, qg_sem, out_sem, dq_send, dq_recv, g_send, g_recv,
    s1_send, s1_recv, s2_send, s2_recv, z_send, z_recv, cx_send, cx_recv, cz_send, cz_recv,
):
    rank = lax.axis_index("dp")
    lane = lax.axis_index("tensor")
    z, x = rank // NX, rank % NX
    y, c = lane // 2, lane % 2

    def at(dz=0, dx=0, dy=0, dc=0):
        return (
            (z + dz) % NZ * NX + (x + dx) % NX,
            (y + dy) % NY * 2 + (c + dc) % 2,
        )

    def tensor_of(dy, dc):
        return (y + dy) % NY * 2 + (c + dc) % 2

    def remote(src, dst, send, recv, device):
        return pltpu.make_async_remote_copy(
            src_ref=src, dst_ref=dst, send_sem=send, recv_sem=recv, device_id=device,
            device_id_type=MESH,
        )

    def head_lanes(head):
        return pl.ds(pl.multiple_of(head * HD, HD), HD)

    def qg_copies(head):
        lanes = head_lanes(head)
        return [
            pltpu.make_async_copy(q_hbm.at[:, :, lanes], q_ref.at[:, :, lanes], qg_sem.at[0, head]),
            pltpu.make_async_copy(g_hbm.at[:, :, lanes], g_ref.at[:, :, lanes], qg_sem.at[1, head]),
        ]

    k_copy = pltpu.make_async_copy(k_hbm, k_ref, in_sem.at[0])
    v_copy = pltpu.make_async_copy(v_hbm, v_ref, in_sem.at[1])
    x_copy = pltpu.make_async_copy(x_hbm, x_ref, in_sem.at[2])
    k_copy.start()
    for copy in qg_copies(0):
        copy.start()
    v_copy.start()
    for head in range(1, GROUP):
        for copy in qg_copies(head):
            copy.start()
    x_copy.start()

    barrier = pltpu.get_barrier_semaphore()
    peers = [at(dz=j) for j in range(1, NZ)] + [at(dx=j) for j in range(1, NX)]
    peers += [at(dc=1), at(dy=1), at(dy=-1)]
    for peer in peers:
        pl.semaphore_signal(barrier, inc=1, device_id=peer, device_id_type=MESH)
    pl.semaphore_wait(barrier, len(peers))

    tokens = jnp.int32(0)
    for row in range(ROWS):
        for doc in range(DOCS):
            tokens = tokens + lengths_ref[row, doc]
    count_ref[...] = jnp.full((8, 128), tokens, jnp.int32).astype(f32)

    def count_x(j):
        return remote(count_ref, cx_ref.at[j - 1], cx_send.at[j - 1], cx_recv.at[j - 1], at(dx=j))

    def count_z(j):
        return remote(plane_ref, cz_ref.at[j - 1], cz_send.at[j - 1], cz_recv.at[j - 1], at(dz=j))

    for j in range(1, NX):
        count_x(j).start()

    def dq_copy(qb, head):
        lanes = head_lanes(head)
        piece = head * BLOCKS + qb
        return remote(
            dq_ref.at[0, pl.ds(qb * BQ, BQ), lanes],
            dq_hbm.at[1, pl.ds(qb * BQ, BQ), lanes],
            dq_send.at[piece], dq_recv.at[piece], at(dz=NZ // 2),
        )

    def kept_copy():
        return pltpu.make_async_copy(dq_ref.at[1], dq_hbm.at[0], out_sem.at[0])

    def kv_copy(group, index, block, half, device):
        slot, kb = group // BLOCKS, BLOCKS - 1 - group % BLOCKS
        columns = pl.ds(pl.multiple_of(kb * BQ, BQ), BQ)
        features = pl.ds(0, FEATURES) if half is None else pl.ds(half * HD, HD)
        ref = kv_ref.at[slot, block, features, columns]
        return remote(ref, ref, g_send.at[group, index], g_recv.at[group, index], device)

    up, down, other = at(dy=1), at(dy=-1), at(dc=1)

    def own_copies(group):
        mine = tensor_of(0, 0)
        return [
            kv_copy(group, 1, mine, None, up),
            kv_copy(group, 2, mine, None, down),
            kv_copy(group, 0, mine, None, other),
        ]

    def from_below(group):
        return kv_copy(group, 1, tensor_of(-1, 0), None, up)

    def from_above(group):
        return kv_copy(group, 2, tensor_of(1, 0), None, down)

    def forward_copies(group):
        return [
            kv_copy(group, 3, tensor_of(-1, 0), 0, up),
            kv_copy(group, 4, tensor_of(1, 0), 1, down),
            kv_copy(group, 5, tensor_of(-1, 0), None, other),
            kv_copy(group, 6, tensor_of(1, 0), None, other),
        ]

    def far_arrivals(group):
        return [
            kv_copy(group, 3, tensor_of(2, 0), 0, up),
            kv_copy(group, 4, tensor_of(2, 0), 1, down),
        ]

    def far_copies(group):
        return [
            kv_copy(group, 7, tensor_of(2, 0), 0, other),
            kv_copy(group, 8, tensor_of(2, 0), 1, other),
        ]

    def stage_forward(group):
        from_below(group).wait_recv()
        from_above(group).wait_recv()
        for copy in forward_copies(group):
            copy.start()

    def stage_far(group):
        for copy in far_arrivals(group):
            copy.wait_recv()
        for copy in far_copies(group):
            copy.start()

    k_copy.wait()
    v_copy.wait()

    @pl.loop(0, ROWS)
    def _(slot):
        row = order_ref[0, slot]
        kt_ref[...] = k_ref[row].astype(f32).T.astype(bf16)
        dk_ref[...] = jnp.zeros_like(dk_ref)
        dv_ref[...] = jnp.zeros_like(dv_ref)
        ends = []
        running = jnp.int32(0)
        for doc in range(DOCS):
            running = running + lengths_ref[row, doc]
            ends.append(running)
        for qb in reversed(range(BLOCKS)):
            group = slot * BLOCKS + (BLOCKS - 1 - qb)
            tokens_here = slice(qb * BQ, qb * BQ + BQ)

            @pl.loop(0, GROUP)
            def _(head, qb=qb, tokens_here=tokens_here):
                lanes = head_lanes(head)
                if qb == BLOCKS - 1:

                    @pl.when(slot == 0)
                    def _():
                        for copy in qg_copies(head):
                            copy.wait()

                query = jnp.where(
                    row == 0, q_ref[0, tokens_here, lanes], q_ref[1, tokens_here, lanes]
                )
                grad = jnp.where(
                    row == 0, g_ref[0, tokens_here, lanes], g_ref[1, tokens_here, lanes]
                )
                dq_ref[slot, tokens_here, lanes] = attend_block(
                    qb, query, grad,
                    k_ref, v_ref, kt_ref, row, ends, dk_ref, dv_ref,
                )

                @pl.when(slot == 0)
                def _():
                    dq_copy(qb, head).start()

            pair = jnp.concatenate(
                [dk_ref[tokens_here, :] * score_scale, dv_ref[tokens_here, :]], axis=1
            )
            kv_ref[slot, tensor_of(0, 0), :, tokens_here] = pair.T.astype(bf16)
            for copy in own_copies(group):
                copy.start()

            @pl.when(group >= 1)
            def _(group=group):
                stage_forward(group - 1)

            @pl.when(group >= 2)
            def _(group=group):
                stage_far(group - 2)

    kept_copy().start()
    for j in range(1, NX):
        count_x(j).wait()
    plane_ref[...] = count_ref[...] + cx_ref[0] + cx_ref[1] + cx_ref[2]
    for j in range(1, NZ):
        count_z(j).start()
    x_copy.wait()
    groups = ROWS * BLOCKS

    def block_of(i):
        shift = jnp.where(i < 2, 0, jnp.where(i < 4, 1, jnp.where(i < 6, 3, 2)))
        return (y + shift) % NY * 2 + (c + i) % 2

    def s1_copy(i, way):
        return remote(
            s1_ref.at[i, way], r1_ref.at[i, way], s1_send.at[i, way], s1_recv.at[i, way],
            at(dx=1 if way == 0 else -1),
        )

    def s2_copy(i, way):
        return remote(
            s2_ref.at[i, way], r2_ref.at[i, way], s2_send.at[i, way], s2_recv.at[i, way],
            at(dx=1 if way == 0 else -1),
        )

    def z_copy(i):
        block = block_of(i)
        return remote(
            zs_ref.at[i], zr_ref.at[z], z_send.at[i], z_recv.at[z], (block * NX + x, lane)
        )

    def part(i, dx, first=0, size=PART):
        begin = pl.multiple_of((x + dx) % NX * PART + first, HALF)
        return wt_ref[i, pl.ds(begin, size), :]

    first_row, second_row = order_ref[0, 0], order_ref[0, 1]

    @pl.loop(0, NT + LAG_C)
    def _(step):
        @pl.when(step == 1)
        def _():
            @pl.loop(0, groups)
            def _(group):
                kv_copy(group, 0, tensor_of(0, 1), None, other).wait_recv()

        @pl.when(step == 2)
        def _():
            stage_forward(groups - 1)
            stage_far(groups - 2)

        @pl.when(step == 3)
        def _():
            @pl.loop(0, groups)
            def _(group):
                kv_copy(group, 6, tensor_of(1, 1), None, other).wait_recv()

        @pl.when(step == 4)
        def _():
            stage_far(groups - 1)

        @pl.when(step == 5)
        def _():
            @pl.loop(0, groups)
            def _(group):
                kv_copy(group, 5, tensor_of(-1, 1), None, other).wait_recv()

        @pl.when(step == 7)
        def _():
            @pl.loop(0, groups)
            def _(group):
                kv_copy(group, 7, tensor_of(2, 1), 0, other).wait_recv()
                kv_copy(group, 8, tensor_of(2, 1), 1, other).wait_recv()

        @pl.when(step < NT)
        def _():
            block = block_of(step)
            wt_ref[step] = jnp.dot(
                kv_ref[0, block], x_ref[first_row], preferred_element_type=f32
            ) + jnp.dot(kv_ref[1, block], x_ref[second_row], preferred_element_type=f32)
            s1_ref[step, 0] = part(step, 2, 0, HALF).astype(bf16)
            s1_ref[step, 1] = part(step, 2, HALF, HALF).astype(bf16)
            s1_copy(step, 0).start()
            s1_copy(step, 1).start()

        @pl.when((step >= LAG_B) & (step < NT + LAG_B))
        def _():
            i = step - LAG_B
            s1_copy(i, 0).wait_recv()
            s1_copy(i, 1).wait_recv()
            s2_ref[i, 0, :HALF] = (part(i, 1, 0, HALF) + r1_ref[i, 0].astype(f32)).astype(bf16)
            s2_ref[i, 0, HALF:] = part(i, 1, HALF, HALF).astype(bf16)
            s2_ref[i, 1, :HALF] = part(i, -1, 0, HALF).astype(bf16)
            s2_ref[i, 1, HALF:] = (part(i, -1, HALF, HALF) + r1_ref[i, 1].astype(f32)).astype(bf16)
            s2_copy(i, 0).start()
            s2_copy(i, 1).start()

        @pl.when(step >= LAG_C)
        def _():
            i = step - LAG_C
            s2_copy(i, 0).wait_recv()
            s2_copy(i, 1).wait_recv()
            reduced = part(i, 0) + r2_ref[i, 0].astype(f32) + r2_ref[i, 1].astype(f32)

            @pl.when(block_of(i) == z)
            def _():
                w_ref[...] = reduced

            @pl.when(block_of(i) != z)
            def _():
                zs_ref[i] = reduced.astype(bf16)
                z_copy(i).start()

    total = plane_ref[...]
    for j in range(1, NZ):
        count_z(j).wait()
    for j in range(1, NZ):
        total = total + cz_ref[j - 1]
    scale = loss_scale / total[0:1, 0:1]

    @pl.loop(1, NZ)
    def _(j):
        source = (z + j) % NZ
        remote(
            zs_ref.at[0], zr_ref.at[source], z_send.at[0], z_recv.at[source], at(dz=j)
        ).wait_recv()
        w_ref[...] += zr_ref[source].astype(f32)

    w_ref[...] = w_ref[...] * scale

    @pl.loop(0, NT)
    def _(i):
        for way in range(2):
            s1_copy(i, way).wait_send()
            s2_copy(i, way).wait_send()

        @pl.when(block_of(i) != z)
        def _():
            z_copy(i).wait_send()

    @pl.loop(0, groups)
    def _(group):
        for copy in own_copies(group) + forward_copies(group) + far_copies(group):
            copy.wait_send()

    kept_copy().wait()

    @pl.loop(0, GROUP)
    def _(head):
        for qb in range(BLOCKS):
            dq_copy(qb, head).wait()


def shards(
    layer_input, query_states, key_states, value_states, output_grad, doc_lengths, send_order
):
    def by_rows(array_in):
        return array_in.reshape(ROWS, ROW_LEN, array_in.shape[-1])

    anywhere = pl.BlockSpec(memory_space=pl.ANY)
    scalars = pl.BlockSpec(memory_space=pltpu.SMEM)
    dma = pltpu.SemaphoreType.DMA
    query_grad, weight_grad = pl.pallas_call(
        whole_kernel,
        out_shape=(
            jax.ShapeDtypeStruct((ROWS, ROW_LEN, WIDTH), bf16),
            jax.ShapeDtypeStruct((PART, WIDTH), f32),
        ),
        in_specs=[scalars, scalars] + [anywhere] * 5,
        out_specs=[anywhere, pl.BlockSpec(memory_space=pltpu.VMEM)],
        scratch_shapes=[
            pltpu.VMEM((ROWS, ROW_LEN, WIDTH), bf16),
            pltpu.VMEM((ROWS, ROW_LEN, WIDTH), bf16),
            pltpu.VMEM((ROWS, ROW_LEN, HD), bf16),
            pltpu.VMEM((ROWS, ROW_LEN, HD), bf16),
            pltpu.VMEM((ROWS, ROW_LEN, WIDTH), bf16),
            pltpu.VMEM((HD, ROW_LEN), bf16),
            pltpu.VMEM((ROW_LEN, HD), f32),
            pltpu.VMEM((ROW_LEN, HD), f32),
            pltpu.VMEM((ROWS, ROW_LEN, WIDTH), bf16),
            pltpu.VMEM((ROWS, NT, FEATURES, ROW_LEN), bf16),
            pltpu.VMEM((NT, FEATURES, WIDTH), f32),
            pltpu.VMEM((NT, 2, HALF, WIDTH), bf16),
            pltpu.VMEM((NT, 2, HALF, WIDTH), bf16),
            pltpu.VMEM((NT, 2, PART, WIDTH), bf16),
            pltpu.VMEM((NT, 2, PART, WIDTH), bf16),
            pltpu.VMEM((NT, PART, WIDTH), bf16),
            pltpu.VMEM((NZ, PART, WIDTH), bf16),
            pltpu.VMEM((8, 128), f32),
            pltpu.VMEM((NX - 1, 8, 128), f32),
            pltpu.VMEM((8, 128), f32),
            pltpu.VMEM((NZ - 1, 8, 128), f32),
            dma((3,)),
            dma((2, GROUP)),
            dma((1,)),
            dma((GROUP * BLOCKS,)),
            dma((GROUP * BLOCKS,)),
            dma((ROWS * BLOCKS, 9)),
            dma((ROWS * BLOCKS, 9)),
            dma((NT, 2)),
            dma((NT, 2)),
            dma((NT, 2)),
            dma((NT, 2)),
            dma((NT,)),
            dma((NZ,)),
            dma((NX - 1,)),
            dma((NX - 1,)),
            dma((NZ - 1,)),
            dma((NZ - 1,)),
        ],
        compiler_params=pltpu.CompilerParams(
            collective_id=0, has_side_effects=True, vmem_limit_bytes=60 << 20
        ),
        name="attention_backward_and_weight_grad",
    )(
        send_order,
        doc_lengths,
        by_rows(layer_input),
        by_rows(query_states),
        by_rows(key_states),
        by_rows(value_states),
        by_rows(output_grad),
    )
    return (query_grad.reshape(-1, WIDTH), weight_grad)


def solution(mesh):
    placed = (P("dp", "tensor"),) * 5 + (P("dp", None),) * 2
    return jax.shard_map(
        shards,
        mesh=mesh,
        in_specs=placed,
        out_specs=(P("dp", "tensor"), P("dp", "tensor")),
        check_vma=False,
    )
```

time: 384 us -> 102 us (0.27)
  the two profiles are of different devices: /device:TPU:25 before, /device:TPU:17 now
where the time goes in v2:
time: 102 us
  Pallas kernels  97.5 us (96%)
  local copies, waits for them, and re-layouts  4.16 us (4%)
    pallas_call x1, Pallas kernels, shards(): pl.pallas_call(whole_kernel, out_shape=(jax.ShapeDtypeStruct((ROWS, ROW_L...  97.5 us
    unnamed x4, local copies, waits for them, and re-layouts  4.16 us

profile of v2, /device:TPU:17, one launch (start us, length us, event | category | flops | bytes accessed | tf_op | source)
XLA Modules:
  0.0 102.4 jit_solution(1588134483263030450)
XLA Ops:
  0.6 97.5 %attention_backward_and_weight_grad.1 = (bf16[2,1024,640]{2,1,0:T(8,128)(2,1)}, f32[64,640]{1,0:T(8,128)}) custom-call(s32[1,2]{1,0:T(1,128)} %order_ref.1, s32[2,8]{1,0:T(2,128)} %lengths_ref.1, bf16[2,1024,640]{2,1,0:T(8,128)(2,1)} %bitcast.6, bf16[2,1024,640]{2,1,0:T(8,128)(2,1)} %bitcast.7, bf16[2,1024,128]{2,1,0:T(8,128)(2,1)} %bitcast.10, ...), custom_call_target="tpu_custom_call" | custom-call | tf_op jit(solution)/shard_map/attention_backward_and_weight_grad/pallas_call | solution.py:427
  98.2 0.0 copy-start
  98.2 3.5 %copy.11 = bf16[2048,640]{1,0:T(8,128)(2,1)} copy(bf16[2048,640]{1,0:T(8,128)(2,1)} %bitcast.9) | data formatting | bytes 5242880
  101.7 0.0 copy-done
  101.7 0.7 copy.12
Async XLA Ops:
  98.2 3.5 %copy-start = (f32[64,640]{1,0:T(8,128)S(1)}, f32[64,640]{1,0:T(8,128)}, u32[]{:S(2)}) copy-start(f32[64,640]{1,0:T(8,128)} %get-tuple-element.9) | copy-start | bytes 491524

commit v3 on v2

--- a/solution.py
+++ b/solution.py
@@ -22,48 +22,87 @@
 FEATURES = 2 * HD
 PART = FEATURES // NX
 HALF = PART // 2
-LAG_B = 2
-LAG_C = 4
+LAG_B = 1
+LAG_C = 3
 
 loss_scale = 256.0
 masked_score = -1e30
 score_scale = HD ** (-0.5)
 exp_scale = score_scale * math.log2(math.e)
 MESH = pl.DeviceIdType.MESH
+DURING = {5: ((0, 0), (0, 1), (0, 2)), 6: ((1, 0),), 7: ((0, 3), (1, 1), (1, 2))}
 f32 = jnp.float32
 bf16 = jnp.bfloat16
 
 
-def attend_block(qb, query, grad, k_ref, v_ref, kt_ref, row, ends, dk_ref, dv_ref):
+def dot_nt(left, right):
+    return lax.dot_general(left, right, (((1,), (1,)), ((), ())), preferred_element_type=f32)
+
+
+def first_pass(offset, diagonal, scores, grad_probs, start, query_index):
+    key_index = lax.broadcasted_iota(jnp.int32, (BQ, BQ), 0)
+    allowed = key_index >= start - offset
+    if diagonal:
+        allowed = allowed & (key_index <= query_index - offset)
+    scores = jnp.where(allowed, scores, masked_score)
+    top = jnp.max(scores, axis=0, keepdims=True)
+    exponent = jnp.exp2((scores - top) * exp_scale)
+    return (
+        exponent,
+        grad_probs,
+        top,
+        jnp.sum(exponent, axis=0, keepdims=True),
+        jnp.sum(exponent * grad_probs, axis=0, keepdims=True),
+    )
+
+
+def tile_scales(parts, live):
+    top = parts[0][2]
+    for part in parts[1:]:
+        top = jnp.maximum(top, part[2])
+    shift = [jnp.exp2((part[2] - top) * exp_scale) for part in parts]
+    total = sum(by * part[3] for by, part in zip(shift, parts))
+    weighted = sum(by * part[4] for by, part in zip(shift, parts))
+    inverse = live / total
+    return [inverse * by for by in shift], weighted / total
+
+
+def attend_group(qb, load, k_ref, v_ref, kt_ref, row, ends, dk_ref, dv_ref, store):
     q_first = qb * BQ
-    length = q_first + BQ
-    scores = lax.dot_general(
-        k_ref[row, :length, :], query, (((1,), (1,)), ((), ())), preferred_element_type=f32
-    )
     query_index = lax.broadcasted_iota(jnp.int32, (1, BQ), 1) + q_first
     start = jnp.zeros((1, BQ), jnp.int32)
     for end in ends:
         start = jnp.where(query_index >= end, end, start)
     live = jnp.where(query_index < ends[-1], 1.0, 0.0).astype(f32)
-    key_index = lax.broadcasted_iota(jnp.int32, (length, BQ), 0)
-    allowed = (key_index >= start) & (key_index <= query_index)
-    scores = jnp.where(allowed, scores, masked_score)
-    top = jnp.max(scores, axis=0, keepdims=True)
-    exponent = jnp.exp2((scores - top) * exp_scale)
-    total = jnp.sum(exponent, axis=0, keepdims=True)
-    grad_probs = lax.dot_general(
-        v_ref[row, :length, :], grad, (((1,), (1,)), ((), ())), preferred_element_type=f32
-    )
-    weighted = jnp.sum(exponent * grad_probs, axis=0, keepdims=True)
-    inverse = live / total
-    delta = weighted / total
-    probs = exponent * inverse
-    probs_low = probs.astype(bf16)
-    grad_scores = (probs * (grad_probs - delta)).astype(bf16)
-    dv_ref[:length, :] += jnp.dot(probs_low, grad, preferred_element_type=f32)
-    dk_ref[:length, :] += jnp.dot(grad_scores, query, preferred_element_type=f32)
-    dq_t = jnp.dot(kt_ref[:, :length], grad_scores, preferred_element_type=f32)
-    return (dq_t.T * score_scale).astype(bf16)
+    before = None
+    for head in range(GROUP + 1):
+        now = None
+        if head < GROUP:
+            query, grad = load(head)
+            now = (query, grad, [])
+        if before is not None:
+            scales, delta = tile_scales(before[2], live)
+            dq_t = jnp.zeros((HD, BQ), f32)
+        for tile in range(qb + 1):
+            keys = slice(tile * BQ, tile * BQ + BQ)
+            if now is not None:
+                scores = dot_nt(k_ref[row, keys, :], query)
+                grad_probs = dot_nt(v_ref[row, keys, :], grad)
+            if before is not None:
+                probs = before[2][tile][0] * scales[tile]
+                grad_scores = (probs * (before[2][tile][1] - delta)).astype(bf16)
+                dv_ref[keys, :] += jnp.dot(
+                    probs.astype(bf16), before[1], preferred_element_type=f32
+                )
+                dk_ref[keys, :] += jnp.dot(grad_scores, before[0], preferred_element_type=f32)
+                dq_t = dq_t + jnp.dot(kt_ref[:, keys], grad_scores, preferred_element_type=f32)
+            if now is not None:
+                now[2].append(
+                    first_pass(tile * BQ, tile == qb, scores, grad_probs, start, query_index)
+                )
+        if before is not None:
+            store(head - 1, (dq_t.T * score_scale).astype(bf16))
+        before = now
 
 
 def whole_kernel(
@@ -95,6 +134,8 @@
         )
 
     def head_lanes(head):
+        if isinstance(head, int):
+            return pl.ds(head * HD, HD)
         return pl.ds(pl.multiple_of(head * HD, HD), HD)
 
     def qg_copies(head):
@@ -152,9 +193,8 @@
 
     def kv_copy(group, index, block, half, device):
         slot, kb = group // BLOCKS, BLOCKS - 1 - group % BLOCKS
-        columns = pl.ds(pl.multiple_of(kb * BQ, BQ), BQ)
         features = pl.ds(0, FEATURES) if half is None else pl.ds(half * HD, HD)
-        ref = kv_ref.at[slot, block, features, columns]
+        ref = kv_ref.at[slot, kb, block, features]
         return remote(ref, ref, g_send.at[group, index], g_recv.at[group, index], device)
 
     up, down, other = at(dy=1), at(dy=-1), at(dc=1)
@@ -208,8 +248,7 @@
     k_copy.wait()
     v_copy.wait()
 
-    @pl.loop(0, ROWS)
-    def _(slot):
+    for slot in range(ROWS):
         row = order_ref[0, slot]
         kt_ref[...] = k_ref[row].astype(f32).T.astype(bf16)
         dk_ref[...] = jnp.zeros_like(dk_ref)
@@ -223,45 +262,30 @@
             group = slot * BLOCKS + (BLOCKS - 1 - qb)
             tokens_here = slice(qb * BQ, qb * BQ + BQ)
 
-            @pl.loop(0, GROUP)
-            def _(head, qb=qb, tokens_here=tokens_here):
-                lanes = head_lanes(head)
-                if qb == BLOCKS - 1:
-
-                    @pl.when(slot == 0)
-                    def _():
-                        for copy in qg_copies(head):
-                            copy.wait()
-
-                query = jnp.where(
-                    row == 0, q_ref[0, tokens_here, lanes], q_ref[1, tokens_here, lanes]
+            def load(head):
+                lanes = slice(head * HD, head * HD + HD)
+                if slot == 0 and qb == BLOCKS - 1:
+                    for copy in qg_copies(head):
+                        copy.wait()
+                return (
+                    jnp.where(row == 0, q_ref[0, tokens_here, lanes], q_ref[1, tokens_here, lanes]),
+                    jnp.where(row == 0, g_ref[0, tokens_here, lanes], g_ref[1, tokens_here, lanes]),
                 )
-                grad = jnp.where(
-                    row == 0, g_ref[0, tokens_here, lanes], g_ref[1, tokens_here, lanes]
-                )
-                dq_ref[slot, tokens_here, lanes] = attend_block(
-                    qb, query, grad,
-                    k_ref, v_ref, kt_ref, row, ends, dk_ref, dv_ref,
-                )
-
-                @pl.when(slot == 0)
-                def _():
+
+            def store(head, piece):
+                dq_ref[slot, tokens_here, head * HD : head * HD + HD] = piece
+                if slot == 0:
                     dq_copy(qb, head).start()
 
+            attend_group(qb, load, k_ref, v_ref, kt_ref, row, ends, dk_ref, dv_ref, store)
             pair = jnp.concatenate(
                 [dk_ref[tokens_here, :] * score_scale, dv_ref[tokens_here, :]], axis=1
             )
-            kv_ref[slot, tensor_of(0, 0), :, tokens_here] = pair.T.astype(bf16)
+            kv_ref[slot, qb, tensor_of(0, 0)] = pair.T.astype(bf16)
             for copy in own_copies(group):
                 copy.start()
-
-            @pl.when(group >= 1)
-            def _(group=group):
-                stage_forward(group - 1)
-
-            @pl.when(group >= 2)
-            def _(group=group):
-                stage_far(group - 2)
+            for stage, ready in DURING.get(group, ()):
+                (stage_forward if stage == 0 else stage_far)(ready)
 
     kept_copy().start()
     for j in range(1, NX):
@@ -300,56 +324,38 @@
 
     first_row, second_row = order_ref[0, 0], order_ref[0, 1]
 
-    @pl.loop(0, NT + LAG_C)
+    def own_part(step):
+        i = jnp.where(step < 2, step, step - 2)
+        return i, (step >= 0) & (i < NT) & ((step < 2) | (step >= 4))
+
+    def gathered(slot, block):
+        return jnp.concatenate([kv_ref[slot, kb, block] for kb in range(BLOCKS)], axis=1)
+
+    def wait_group(index, block, half=None):
+        @pl.loop(0, groups)
+        def _(group):
+            kv_copy(group, index, block, half, other).wait_recv()
+
+    @pl.loop(0, NT + 2 + LAG_C)
     def _(step):
-        @pl.when(step == 1)
-        def _():
-            @pl.loop(0, groups)
-            def _(group):
-                kv_copy(group, 0, tensor_of(0, 1), None, other).wait_recv()
-
-        @pl.when(step == 2)
-        def _():
-            stage_forward(groups - 1)
-            stage_far(groups - 2)
-
-        @pl.when(step == 3)
-        def _():
-            @pl.loop(0, groups)
-            def _(group):
-                kv_copy(group, 6, tensor_of(1, 1), None, other).wait_recv()
-
-        @pl.when(step == 4)
-        def _():
-            stage_far(groups - 1)
-
-        @pl.when(step == 5)
-        def _():
-            @pl.loop(0, groups)
-            def _(group):
-                kv_copy(group, 5, tensor_of(-1, 1), None, other).wait_recv()
-
-        @pl.when(step == 7)
-        def _():
-            @pl.loop(0, groups)
-            def _(group):
-                kv_copy(group, 7, tensor_of(2, 1), 0, other).wait_recv()
-                kv_copy(group, 8, tensor_of(2, 1), 1, other).wait_recv()
-
-        @pl.when(step < NT)
-        def _():
-            block = block_of(step)
-            wt_ref[step] = jnp.dot(
-                kv_ref[0, block], x_ref[first_row], preferred_element_type=f32
-            ) + jnp.dot(kv_ref[1, block], x_ref[second_row], preferred_element_type=f32)
-            s1_ref[step, 0] = part(step, 2, 0, HALF).astype(bf16)
-            s1_ref[step, 1] = part(step, 2, HALF, HALF).astype(bf16)
-            s1_copy(step, 0).start()
-            s1_copy(step, 1).start()
-
-        @pl.when((step >= LAG_B) & (step < NT + LAG_B))
-        def _():
-            i = step - LAG_B
+        i_a, go_a = own_part(step)
+
+        @pl.when(go_a)
+        def _():
+            block = block_of(i_a)
+            wt_ref[i_a] = jnp.dot(
+                gathered(0, block), x_ref[first_row], preferred_element_type=f32
+            ) + jnp.dot(gathered(1, block), x_ref[second_row], preferred_element_type=f32)
+            s1_ref[i_a, 0] = part(i_a, 2, 0, HALF).astype(bf16)
+            s1_ref[i_a, 1] = part(i_a, 2, HALF, HALF).astype(bf16)
+            s1_copy(i_a, 0).start()
+            s1_copy(i_a, 1).start()
+
+        i_b, go_b = own_part(step - LAG_B)
+
+        @pl.when(go_b)
+        def _():
+            i = i_b
             s1_copy(i, 0).wait_recv()
             s1_copy(i, 1).wait_recv()
             s2_ref[i, 0, :HALF] = (part(i, 1, 0, HALF) + r1_ref[i, 0].astype(f32)).astype(bf16)
@@ -359,9 +365,11 @@
             s2_copy(i, 0).start()
             s2_copy(i, 1).start()
 
-        @pl.when(step >= LAG_C)
-        def _():
-            i = step - LAG_C
+        i_c, go_c = own_part(step - LAG_C)
+
+        @pl.when(go_c)
+        def _():
+            i = i_c
             s2_copy(i, 0).wait_recv()
             s2_copy(i, 1).wait_recv()
             reduced = part(i, 0) + r2_ref[i, 0].astype(f32) + r2_ref[i, 1].astype(f32)
@@ -374,6 +382,44 @@
             def _():
                 zs_ref[i] = reduced.astype(bf16)
                 z_copy(i).start()
+
+        @pl.when(step == 0)
+        def _():
+            wait_group(0, tensor_of(0, 1))
+
+        @pl.when(step == 1)
+        def _():
+            stage_forward(4)
+            stage_far(3)
+
+        @pl.when(step == 2)
+        def _():
+            stage_forward(5)
+            stage_far(4)
+            stage_forward(6)
+
+        @pl.when(step == 3)
+        def _():
+            stage_far(5)
+            stage_forward(7)
+
+        @pl.when(step == 4)
+        def _():
+            stage_far(6)
+            wait_group(6, tensor_of(1, 1))
+
+        @pl.when(step == 5)
+        def _():
+            stage_far(7)
+
+        @pl.when(step == 6)
+        def _():
+            wait_group(5, tensor_of(-1, 1))
+
+        @pl.when(step == 8)
+        def _():
+            wait_group(7, tensor_of(2, 1), 0)
+            wait_group(8, tensor_of(2, 1), 1)
 
     total = plane_ref[...]
     for j in range(1, NZ):
@@ -442,7 +488,7 @@
             pltpu.VMEM((ROW_LEN, HD), f32),
             pltpu.VMEM((ROW_LEN, HD), f32),
             pltpu.VMEM((ROWS, ROW_LEN, WIDTH), bf16),
-            pltpu.VMEM((ROWS, NT, FEATURES, ROW_LEN), bf16),
+            pltpu.VMEM((ROWS, BLOCKS, NT, FEATURES, BQ), bf16),
             pltpu.VMEM((NT, FEATURES, WIDTH), f32),
             pltpu.VMEM((NT, 2, HALF, WIDTH), bf16),
             pltpu.VMEM((NT, 2, HALF, WIDTH), bf16),

time: 102 us -> 93.5 us (0.917)
  the two profiles are of different devices: /device:TPU:17 before, /device:TPU:25 now
where the time goes in v3:
time: 93.5 us; the launch traced here: 93.4 us
  Pallas kernels  88.5 us (95%)
  local copies, waits for them, and re-layouts  4.16 us (4%)
    pallas_call x1, Pallas kernels, shards(): pl.pallas_call(whole_kernel, out_shape=(jax.ShapeDtypeStruct((ROWS, ROW_L...  88.5 us
    unnamed x4, local copies, waits for them, and re-layouts  4.16 us

profile of v3, /device:TPU:25, one launch (start us, length us, event | category | flops | bytes accessed | tf_op | source)
XLA Modules:
  0.0 93.4 jit_solution(4131852995954603771)
XLA Ops:
  0.6 88.5 %attention_backward_and_weight_grad.1 = (bf16[2,1024,640]{2,1,0:T(8,128)(2,1)}, f32[64,640]{1,0:T(8,128)}) custom-call(s32[1,2]{1,0:T(1,128)} %order_ref.1, s32[2,8]{1,0:T(2,128)} %lengths_ref.1, bf16[2,1024,640]{2,1,0:T(8,128)(2,1)} %bitcast.6, bf16[2,1024,640]{2,1,0:T(8,128)(2,1)} %bitcast.7, bf16[2,1024,128]{2,1,0:T(8,128)(2,1)} %bitcast.10, ...), custom_call_target="tpu_custom_call" | custom-call | tf_op jit(solution)/shard_map/attention_backward_and_weight_grad/pallas_call | solution.py:473
  89.2 0.0 copy-start
  89.2 3.5 %copy.11 = bf16[2048,640]{1,0:T(8,128)(2,1)} copy(bf16[2048,640]{1,0:T(8,128)(2,1)} %bitcast.9) | data formatting | bytes 5242880
  92.7 0.0 copy-done
  92.7 0.7 copy.12
Async XLA Ops:
  89.2 3.5 %copy-start = (f32[64,640]{1,0:T(8,128)S(1)}, f32[64,640]{1,0:T(8,128)}, u32[]{:S(2)}) copy-start(f32[64,640]{1,0:T(8,128)} %get-tuple-element.9) | copy-start | bytes 491524

commit v4 on v3

--- a/solution.py
+++ b/solution.py
@@ -30,7 +30,7 @@
 score_scale = HD ** (-0.5)
 exp_scale = score_scale * math.log2(math.e)
 MESH = pl.DeviceIdType.MESH
-DURING = {5: ((0, 0), (0, 1), (0, 2)), 6: ((1, 0),), 7: ((0, 3), (1, 1), (1, 2))}
+DURING = {5: ((0, 0), (0, 1), (0, 2)), 6: ((0, 3),), 7: ((0, 4),)}
 f32 = jnp.float32
 bf16 = jnp.bfloat16
 
@@ -258,13 +258,12 @@
         for doc in range(DOCS):
             running = running + lengths_ref[row, doc]
             ends.append(running)
-        for qb in reversed(range(BLOCKS)):
-            group = slot * BLOCKS + (BLOCKS - 1 - qb)
+        for qb in (0, 3, 2, 1) if slot == 0 else (3, 2, 1, 0):
             tokens_here = slice(qb * BQ, qb * BQ + BQ)
 
             def load(head):
                 lanes = slice(head * HD, head * HD + HD)
-                if slot == 0 and qb == BLOCKS - 1:
+                if slot == 0 and qb == 0:
                     for copy in qg_copies(head):
                         copy.wait()
                 return (
@@ -278,12 +277,19 @@
                     dq_copy(qb, head).start()
 
             attend_group(qb, load, k_ref, v_ref, kt_ref, row, ends, dk_ref, dv_ref, store)
-            pair = jnp.concatenate(
-                [dk_ref[tokens_here, :] * score_scale, dv_ref[tokens_here, :]], axis=1
-            )
-            kv_ref[slot, qb, tensor_of(0, 0)] = pair.T.astype(bf16)
-            for copy in own_copies(group):
-                copy.start()
+            final = (qb,)
+            if slot == 0:
+                final = {0: (), 1: (1, 0)}.get(qb, (qb,))
+            group = None
+            for kb in final:
+                group = slot * BLOCKS + (BLOCKS - 1 - kb)
+                keys_here = slice(kb * BQ, kb * BQ + BQ)
+                pair = jnp.concatenate(
+                    [dk_ref[keys_here, :] * score_scale, dv_ref[keys_here, :]], axis=1
+                )
+                kv_ref[slot, kb, tensor_of(0, 0)] = pair.T.astype(bf16)
+                for copy in own_copies(group):
+                    copy.start()
             for stage, ready in DURING.get(group, ()):
                 (stage_forward if stage == 0 else stage_far)(ready)
 
@@ -325,8 +331,8 @@
     first_row, second_row = order_ref[0, 0], order_ref[0, 1]
 
     def own_part(step):
-        i = jnp.where(step < 2, step, step - 2)
-        return i, (step >= 0) & (i < NT) & ((step < 2) | (step >= 4))
+        i = jnp.where(step < 2, step, step - 1)
+        return i, (step >= 0) & (i < NT) & (step != 2)
 
     def gathered(slot, block):
         return jnp.concatenate([kv_ref[slot, kb, block] for kb in range(BLOCKS)], axis=1)
@@ -336,7 +342,7 @@
         def _(group):
             kv_copy(group, index, block, half, other).wait_recv()
 
-    @pl.loop(0, NT + 2 + LAG_C)
+    @pl.loop(0, NT + 1 + LAG_C)
     def _(step):
         i_a, go_a = own_part(step)
 
@@ -385,38 +391,36 @@
 
         @pl.when(step == 0)
         def _():
+            stage_forward(5)
             wait_group(0, tensor_of(0, 1))
 
         @pl.when(step == 1)
         def _():
-            stage_forward(4)
-            stage_far(3)
+            stage_forward(6)
 
         @pl.when(step == 2)
         def _():
-            stage_forward(5)
-            stage_far(4)
-            stage_forward(6)
+            stage_forward(7)
 
         @pl.when(step == 3)
         def _():
-            stage_far(5)
-            stage_forward(7)
+            wait_group(6, tensor_of(1, 1))
 
         @pl.when(step == 4)
         def _():
-            stage_far(6)
-            wait_group(6, tensor_of(1, 1))
+            @pl.loop(0, 5)
+            def _(group):
+                stage_far(group)
 
         @pl.when(step == 5)
         def _():
-            stage_far(7)
-
-        @pl.when(step == 6)
-        def _():
+            @pl.loop(5, groups)
+            def _(group):
+                stage_far(group)
+
             wait_group(5, tensor_of(-1, 1))
 
-        @pl.when(step == 8)
+        @pl.when(step == 7)
         def _():
             wait_group(7, tensor_of(2, 1), 0)
             wait_group(8, tensor_of(2, 1), 1)

time: 93.5 us -> 92.9 us (level)
  no operation moved by 1% of the time
where the time goes in v4:
time: 92.9 us; the launch traced here: 92.8 us
  Pallas kernels  88 us (95%)
  local copies, waits for them, and re-layouts  4.16 us (4%)
    pallas_call x1, Pallas kernels, shards(): pl.pallas_call(whole_kernel, out_shape=(jax.ShapeDtypeStruct((ROWS, ROW_L...  88 us
    unnamed x4, local copies, waits for them, and re-layouts  4.16 us

profile of v4, /device:TPU:25, one launch (start us, length us, event | category | flops | bytes accessed | tf_op | source)
XLA Modules:
  0.0 92.8 jit_solution(6056153290694436561)
XLA Ops:
  0.6 88.0 %attention_backward_and_weight_grad.1 = (bf16[2,1024,640]{2,1,0:T(8,128)(2,1)}, f32[64,640]{1,0:T(8,128)}) custom-call(s32[1,2]{1,0:T(1,128)} %order_ref.1, s32[2,8]{1,0:T(2,128)} %lengths_ref.1, bf16[2,1024,640]{2,1,0:T(8,128)(2,1)} %bitcast.6, bf16[2,1024,640]{2,1,0:T(8,128)(2,1)} %bitcast.7, bf16[2,1024,128]{2,1,0:T(8,128)(2,1)} %bitcast.10, ...), custom_call_target="tpu_custom_call" | custom-call | tf_op jit(solution)/shard_map/attention_backward_and_weight_grad/pallas_call | solution.py:477
  88.6 0.0 copy-start
  88.6 3.5 %copy.11 = bf16[2048,640]{1,0:T(8,128)(2,1)} copy(bf16[2048,640]{1,0:T(8,128)(2,1)} %bitcast.9) | data formatting | bytes 5242880
  92.1 0.0 copy-done
  92.1 0.7 copy.12
Async XLA Ops:
  88.6 3.5 %copy-start = (f32[64,640]{1,0:T(8,128)S(1)}, f32[64,640]{1,0:T(8,128)}, u32[]{:S(2)}) copy-start(f32[64,640]{1,0:T(8,128)} %get-tuple-element.9) | copy-start | bytes 491524
